TPU v7x, 128 devices: a whole 4x4x4 slice. The times are simulated.
128 devices in a mesh: gx: 64 (over y, x, z_hi, core), gy: 2 (over z_lo).
Axes of the slice: x: 4, y: 4, z: 4 (z_hi: 2, z_lo: 2; z = z_hi * 2 + z_lo), core: 2. Of those that a mesh axis runs over, the one named last changes fastest.
Arguments:
- adjoint_in: float32 [3, 1024, 128, 256], P(None, 'gx', 'gy'), may hold values from -6 to 6
- checkpoints: bfloat16 [2, 16384, 3, 2048], P(None, ('gx', 'gy')), may hold values from -4 to 4
- send_owner: int32 [16384], P(('gx', 'gy')), may hold values from 0 to 127, as said below
- receive_rows: int32 [16384], P(('gx', 'gy')), may hold values from 0 to 255, as said below
- block_columns: int32 [4096, 8], P(('gx', 'gy')), may hold values from 0 to 35
- eddy_blocks: bfloat16 [8, 128, 128], replicated, may hold values from -0.1875 to 0.1875
- thrust: float32 [80], replicated, may hold values from 0.4 to 1
- yaw_angle: float32 [80], replicated, may hold values from -0.5 to 0.5
- turbine_place: float32 [3, 80], replicated, may hold values from 0 to 1
- turbine_tile: int32 [80], replicated, may hold values from 0 to 127
- fringe_rows: int32 [128], replicated, may hold values from 0 to 1023, as said below
Outputs:
- adjoint_out: float32 [3, 1024, 128, 256], P(None, 'gx', 'gy')
- control_gradient: float32 [2, 80], replicated
Inputs may be any that keep to these rules, and one draw needn't show every extreme that they name: `send_owner`: each storage tile holds 128 slots; at most 2 of its slots name one owner, exactly 2 for some owners; every owner is named by 128 slots in all. `receive_rows`: for each owner the 128 entries name each row storage*2+rank of a slot sent to it exactly once. `fringe_rows`: distinct rows.
All inputs are finite; a program needn't handle non-finite values.
Results may differ from a plain program's by a relative error of at most 0.00086.
Values may be sent and summed in bfloat16 or wider, within the bound.
A program may use at most 128 MiB of HBM per device.

v0:
```python
import jax
import jax.numpy as jnp
from jax import lax
from jax.sharding import PartitionSpec as P

PB = 128
KB = 8
CAP = 2
NZB = 2
TIME_STEP = 0.25
BASE_VISC = 0.1
EDDY_COEF = 0.5
KERNEL_WIDTH = 1.5
FRINGE_KEEP = 0.5


def padded(block, sides, width):
    for axis, dim in sides:
        count = lax.axis_size(axis)
        forward = [(i, i + 1) for i in range(count - 1)]
        forward.append((count - 1, 0))
        backward = [(target, source) for source, target in forward]
        low = lax.ppermute(
            lax.slice_in_dim(block, block.shape[dim] - width, None, axis=dim), axis, forward
        )
        high = lax.ppermute(lax.slice_in_dim(block, 0, width, axis=dim), axis, backward)
        block = jnp.concatenate([low, block, high], axis=dim)
    return block


def turbine_terms(
    tile_index, thrust, yaw_angle, turbine_place, turbine_tile, width_x, width_y, height
):
    owned_mask = (turbine_tile == tile_index).astype(jnp.float32)
    spread = 2.0 * KERNEL_WIDTH * KERNEL_WIDTH
    along_x = jnp.exp(
        -(
            (jnp.arange(width_x, dtype=jnp.float32)[None, :] - turbine_place[0][:, None] * width_x)
            ** 2
        )
        / spread
    )
    along_y = jnp.exp(
        -(
            (jnp.arange(width_y, dtype=jnp.float32)[None, :] - turbine_place[1][:, None] * width_y)
            ** 2
        )
        / spread
    )
    along_z = jnp.exp(
        -(
            (
                jnp.arange(height, dtype=jnp.float32)[None, :]
                - turbine_place[2][:, None] * (0.5 * height)
            )
            ** 2
        )
        / spread
    )
    plan_kernel = (along_x[:, :, None] * along_y[:, None, :]).reshape(
        along_x.shape[0], width_x * width_y
    )
    cosine = jnp.cos(yaw_angle)
    loading = owned_mask * thrust * cosine * cosine
    drag_field = jnp.dot(
        (plan_kernel * loading[:, None]).T, along_z, precision=lax.Precision.HIGHEST
    )
    return (owned_mask, plan_kernel, along_z, drag_field.reshape(width_x, width_y, height))


def block_selector(columns, width_x):
    count_in = (width_x + 2) * NZB
    picks = (columns[:, :, None] == jnp.arange(count_in, dtype=jnp.int32)[None, None, :]).astype(
        jnp.bfloat16
    )
    return picks.reshape(width_x, NZB, KB, width_x + 2, NZB)


def advance(
    extended,
    forward,
    selector,
    eddy_blocks,
    owned_mask,
    plan_kernel,
    along_z,
    drag_field,
    fringe_scale,
):
    center = extended[:, 1:-1, 1:-1, :]
    east_cells = extended[:, 2:, 1:-1, :]
    west_cells = extended[:, :-2, 1:-1, :]
    north_cells = extended[:, 1:-1, 2:, :]
    south_cells = extended[:, 1:-1, :-2, :]
    zero_plane = jnp.zeros_like(center[..., :1])
    upper_cells = jnp.concatenate([center[..., 1:], zero_plane], axis=3)
    lower_cells = jnp.concatenate([zero_plane, center[..., :-1]], axis=3)
    velocity = forward.astype(jnp.float32)
    laplace = (
        east_cells
        + west_cells
        + north_cells
        + south_cells
        + upper_cells
        + lower_cells
        - 6.0 * center
    )
    advect = 0.5 * (
        velocity[0] * (east_cells - west_cells)
        + velocity[1] * (north_cells - south_cells)
        + velocity[2] * (upper_cells - lower_cells)
    )
    viscous = EDDY_COEF * jnp.sqrt(1.0 + jnp.sum(velocity * velocity, axis=0))
    components, width_x, width_y, height = center.shape
    planes = extended[:, :, 1:-1, :].astype(jnp.bfloat16)
    planes = planes.reshape(components, width_x + 2, width_y, NZB, PB)
    picked = jnp.einsum(
        "xbkqc,aqycz->xbkayz", selector, planes, preferred_element_type=jnp.float32
    ).astype(jnp.bfloat16)
    product = jnp.einsum(
        "xbkayz,kzw->axybw", picked, eddy_blocks, preferred_element_type=jnp.float32
    )
    product = product.reshape(components, width_x, width_y, height)
    update = center + TIME_STEP * (advect + BASE_VISC * laplace + viscous * product)
    drag_term = TIME_STEP * drag_field * velocity[0] * center[0]
    first_only = (jnp.arange(components, dtype=jnp.int32) == 0).astype(jnp.float32)
    update = update - first_only[:, None, None, None] * drag_term[None]
    update = update * fringe_scale[None, :, None, None]
    density = (velocity[0] * velocity[0] * center[0]).reshape(width_x * width_y, height)
    projected = jnp.dot(density, along_z.T, precision=lax.Precision.HIGHEST)
    gradient_part = owned_mask * jnp.sum(plan_kernel.T * projected, axis=0)
    return (update, gradient_part)


def shards(
    adjoint_in,
    checkpoints,
    send_owner,
    receive_rows,
    block_columns,
    eddy_blocks,
    thrust,
    yaw_angle,
    turbine_place,
    turbine_tile,
    fringe_rows,
):
    count_x = lax.axis_size("gx")
    count_y = lax.axis_size("gy")
    tile_count = count_x * count_y
    tile_index = lax.axis_index("gx") * count_y + lax.axis_index("gy")
    components, width_x, width_y, height = adjoint_in.shape
    steps_total = checkpoints.shape[0]
    block_shape = checkpoints.shape[2:]
    owner_ids = jnp.arange(tile_count, dtype=jnp.int32)
    onehot = (send_owner[:, None] == owner_ids[None, :]).astype(jnp.int32)
    slot_rank = jnp.sum(jnp.cumsum(onehot, axis=0) * onehot, axis=1) - 1
    position = send_owner * CAP + slot_rank
    row_ids = jnp.arange(tile_count * CAP, dtype=jnp.int32)
    pack_table = (row_ids[:, None] == position[None, :]).astype(jnp.bfloat16)
    pick_table = (receive_rows[:, None] == row_ids[None, :]).astype(jnp.bfloat16)
    selector = block_selector(block_columns, width_x)
    rows_x = lax.axis_index("gx") * width_x + jnp.arange(width_x, dtype=jnp.int32)
    fringe_hit = jnp.any(rows_x[:, None] == fringe_rows[None, :], axis=1)
    fringe_scale = jnp.where(fringe_hit, FRINGE_KEEP, 1.0).astype(jnp.float32)
    owned_mask, plan_kernel, along_z, drag_field = turbine_terms(
        tile_index, thrust, yaw_angle, turbine_place, turbine_tile, width_x, width_y, height
    )
    adjoint = adjoint_in
    gradient_sum = jnp.zeros((thrust.shape[0],), jnp.float32)
    for step_index in range(steps_total):
        stored = checkpoints[steps_total - 1 - step_index]
        packed = jnp.einsum(
            "rs,scb->rcb", pack_table, stored, preferred_element_type=jnp.float32
        ).astype(jnp.bfloat16)
        arrived = lax.all_to_all(
            packed.reshape((tile_count, CAP) + block_shape),
            ("gx", "gy"),
            split_axis=0,
            concat_axis=0,
            tiled=True,
        )
        arrived = arrived.reshape((tile_count * CAP,) + block_shape)
        forward = jnp.einsum(
            "jr,rcb->cjb", pick_table, arrived, preferred_element_type=jnp.float32
        ).astype(jnp.bfloat16)
        forward = forward.reshape(components, width_x, width_y, height)
        extended = padded(adjoint, (("gx", 1), ("gy", 2)), 1)
        adjoint, gradient_part = advance(
            extended,
            forward,
            selector,
            eddy_blocks,
            owned_mask,
            plan_kernel,
            along_z,
            drag_field,
            fringe_scale,
        )
        gradient_sum = gradient_sum + lax.psum(gradient_part, ("gx", "gy"))
    cosine = jnp.cos(yaw_angle)
    sine = jnp.sin(yaw_angle)
    control_gradient = jnp.stack(
        [
            -0.5 * TIME_STEP * cosine * cosine * gradient_sum,
            TIME_STEP * thrust * sine * cosine * gradient_sum,
        ]
    )
    return (adjoint, control_gradient)


def solution(mesh):
    return jax.shard_map(
        shards,
        mesh=mesh,
        in_specs=(
            P(None, "gx", "gy", None),
            P(None, ("gx", "gy"), None, None),
            P(("gx", "gy")),
            P(("gx", "gy")),
            P(("gx", "gy"), None),
            P(),
            P(),
            P(),
            P(),
            P(),
            P(),
        ),
        out_specs=(P(None, "gx", "gy", None), P()),
        check_vma=False,
    )
```

profile of v0, /device:TPU:1, one launch (start us, length us, event | category | flops | bytes accessed | tf_op | source)
XLA Modules:
  0.0 342.7 jit_solution(4182224922127656898)
XLA Ops:
  3.1 4.0 %convolution_convert_fusion.1 = bf16[256,3,2048]{2,0,1:T(8,128)(2,1)} fusion(bf16[2,128,3,2048]{3,1,2,0:T(8,128)(2,1)} %param.12, s32[128]{0:T(128)S(1)} %add_add_fusion), kind=kOutput, calls=%fused_computation.11 | convolution fusion | flops 404258816 | bytes 4719104 | tf_op jit(solution)/shard_map/rs,scb->rcb/dot_general | solution.py:173
  7.1 4.6 %reshape.194 = bf16[128,2,3,2048]{3,1,0,2:T(2,128)(2,1)S(1)} reshape(bf16[256,3,2048]{2,0,1:T(8,128)(2,1)} %convolution_convert_fusion.1) | data formatting | bytes 6291456 | tf_op jit(solution)/shard_map/reshape | solution.py:177
  11.7 3.8 %copy.121 = bf16[128,2,3,2048]{3,1,2,0:T(2,128)(2,1)} copy(bf16[128,2,3,2048]{3,1,0,2:T(2,128)(2,1)S(1)} %reshape.194) | data formatting | bytes 6291456 | tf_op jit(solution)/shard_map/reshape | solution.py:177
  15.6 11.9 %all-to-all-start = ((bf16[128,2,3,2048]{3,1,2,0:T(2,128)(2,1)}), bf16[128,2,3,2048]{3,1,2,0:T(2,128)(2,1)}, u32[]{:S(2)}, u32[]{:S(2)}) async-start(bf16[128,2,3,2048]{3,1,2,0:T(2,128)(2,1)} %copy.121), calls=%async_computation | async-start | bytes 6291456 | tf_op jit(solution)/shard_map/all_to_all | solution.py:176
  28.3 3.5 %collective-permute-start.1 = (f32[3,1,64,256]{3,2,1,0:T(8,128)}, f32[3,1,64,256]{3,2,1,0:T(8,128)}, u32[]{:S(2)}, u32[]{:S(2)}) collective-permute-start(f32[3,1,64,256]{3,2,1,0:T(8,128)} %get-tuple-element.24), channel_id=1, source_target_pairs={{0,2},{2,4},{4,6},{6,8},{8,10},{10,12},{12,14},{14,16},{16,18},{18... | collective-permute-start | bytes 589832 | tf_op jit(solution)/shard_map/ppermute | solution.py:23
  32.0 3.8 %fusion.65 = (f32[3,16,64,255]{3,2,1,0:T(8,128)}, f32[3,16,64,255]{3,2,1,0:T(8,128)}) fusion(f32[3,16,64,256]{3,2,1,0:T(8,128)S(1)} %copy-done.1), kind=kLoop, calls=%fused_computation.124 | loop fusion | bytes 12533760 | tf_op jit(solution)/shard_map/slice | solution.py:96
  35.8 2.6 convolution_convert_fusion
  39.7 2.0 mul.377
  41.8 1.8 multiply_bitcast_fusion.2
  43.6 2.0 copy.160
  45.7 6.0 %reshape.197 = bf16[128,2,3,2048]{3,1,0,2:T(2,128)(2,1)} reshape(bf16[256,3,2048]{2,0,1:T(8,128)(2,1)} %convolution_convert_fusion) | data formatting | bytes 6291456 | tf_op jit(solution)/shard_map/reshape | solution.py:177
  51.7 5.7 %copy.136 = bf16[128,2,3,2048]{3,1,2,0:T(2,128)(2,1)} copy(bf16[128,2,3,2048]{3,1,0,2:T(2,128)(2,1)} %reshape.197) | data formatting | bytes 6291456 | tf_op jit(solution)/shard_map/reshape | solution.py:177
  57.6 8.9 %collective-permute-done.1 = f32[3,1,64,256]{3,2,1,0:T(8,128)} collective-permute-done((f32[3,1,64,256]{3,2,1,0:T(8,128)}, f32[3,1,64,256]{3,2,1,0:T(8,128)}, u32[]{:S(2)}, u32[]{:S(2)}) %collective-permute-start.1) | collective-permute-done | bytes 196640 | tf_op jit(solution)/shard_map/ppermute | solution.py:23
  66.5 1.7 constant_dynamic-update-slice_fusion.2
  68.2 2.5 constant_dynamic-update-slice_fusion.1
  70.8 1.8 constant_dynamic-update-slice_fusion
  74.2 3.5 %concatenate.72 = bf16[3,16,64,2,128]{4,3,2,1,0:T(2,128)(2,1)} reshape(bf16[3,16,64,256]{3,2,1,0:T(8,128)(2,1)} %get-tuple-element.21) | data formatting | bytes 3145728 | tf_op jit(solution)/shard_map/concatenate | solution.py:27
  77.7 4.4 %copy.130 = bf16[3,16,64,2,128]{4,1,3,2,0:T(8,128)(2,1)} copy(bf16[3,16,64,2,128]{4,3,2,1,0:T(2,128)(2,1)} %concatenate.72) | data formatting | bytes 3145728 | tf_op jit(solution)/shard_map/concatenate | solution.py:27
  82.8 5.6 %bitcast_convert_fusion.1 = bf16[16,2,8,3,64,128]{5,2,4,3,1,0:T(8,128)(2,1)S(1)} fusion(bf16[3,1,64,2,128]{4,1,3,2,0:T(2,128)(2,1)} %concatenate.87, bf16[3,16,64,2,128]{4,1,3,2,0:T(8,128)(2,1)} %copy.130, bf16[3,1,64,2,128]{4,1,3,2,0:T(2,128)(2,1)} %concatenate.86, s32[18,2]{0,1:T(2,128)S(1)} %multiply_add_fusion, s32[16,2,8]{2,1,0:T(2,128)S(1)} %bitcast.122), kind=kOutput, calls=%fused_computation.1 | convolution fusion | flops 464593920 | bytes 14353552 | tf_op jit(solution)/shard_map/xbkqc,aqycz->xbkayz/dot_general | solution.py:117
  88.4 3.4 %fusion.14 = f32[3,16,64,2,128]{4,2,0,3,1:T(8,128)S(1)} fusion(bf16[16,2,8,3,64,128]{5,2,4,3,1,0:T(8,128)(2,1)S(1)} %bitcast_convert_fusion.1, bf16[8,128,128]{2,1,0:T(8,128)(2,1)S(1)} %copy-done), kind=kOutput, calls=%fused_computation.40 | convolution fusion | flops 1610612736 | bytes 15990784 | tf_op jit(solution)/shard_map/xbkayz,kzw->axybw/dot_general | solution.py:120
  91.8 4.4 %copy.133 = f32[3,16,64,2,128]{4,3,2,1,0:T(2,128)} copy(f32[3,16,64,2,128]{4,2,0,3,1:T(8,128)S(1)} %fusion.14) | data formatting | bytes 6291456 | tf_op jit(solution)/shard_map/xbkayz,kzw->axybw/transpose | solution.py:120
  96.2 5.5 %reshape.196 = f32[3,16,64,256]{3,2,1,0:T(8,128)} reshape(f32[3,16,64,2,128]{4,3,2,1,0:T(2,128)} %copy.133) | data formatting | bytes 6291456 | tf_op jit(solution)/shard_map/reshape | solution.py:123
  101.8 1.9 fusion.62
  103.7 3.0 collective-permute-start.2
  106.7 10.1 %all-to-all-start.1 = ((bf16[128,2,3,2048]{3,1,2,0:T(2,128)(2,1)}), bf16[128,2,3,2048]{3,1,2,0:T(2,128)(2,1)}, u32[]{:S(2)}, u32[]{:S(2)}) async-start(bf16[128,2,3,2048]{3,1,2,0:T(2,128)(2,1)} %copy.136), calls=%async_computation.1 | async-start | bytes 6291456 | tf_op jit(solution)/shard_map/all_to_all | solution.py:176
  116.8 5.8 %copy.122 = bf16[128,2,3,2048]{3,1,0,2:T(2,128)(2,1)} copy(bf16[128,2,3,2048]{3,1,2,0:T(2,128)(2,1)} %all-to-all-done) | data formatting | bytes 6291456 | tf_op jit(solution)/shard_map/all_to_all | solution.py:176
  122.7 5.7 %reshape.195 = bf16[256,3,2048]{2,0,1:T(8,128)(2,1)} reshape(bf16[128,2,3,2048]{3,1,0,2:T(2,128)(2,1)} %copy.122) | data formatting | bytes 6291456 | tf_op jit(solution)/shard_map/reshape | solution.py:183
  128.4 4.0 %fusion.4 = (f32[2048,128]{1,0:T(8,128)}, bf16[3,2048,128]{2,1,0:T(8,128)(2,1)S(1)}) fusion(bf16[256,3,2048]{2,0,1:T(8,128)(2,1)} %reshape.195, s32[128]{0:T(128)S(1)} %copy-done.8), kind=kOutput, calls=%fused_computation.12 | convolution fusion | flops 405569536 | bytes 5767680 | tf_op jit(solution)/shard_map/jr,rcb->cjb/dot_general | solution.py:184
  132.6 2.1 slice_multiply_fusion.3
  134.7 2.5 copy.124
  137.2 2.4 mul.349
  139.6 2.5 multiply_bitcast_fusion.1
  142.1 3.8 %bitcast_multiply_fusion.1 = (f32[16,64,256]{2,1,0:T(8,128)}, f32[16,64,256]{2,1,0:T(8,128)}) fusion(f32[16,64,256]{2,1,0:T(8,128)} %mul.349, f32[3,16,64,256]{3,2,1,0:T(8,128)S(1)} %copy-done.1, f32[16,64,80]{2,1,0:T(8,128)} %bitcast.121, f32[80]{0:T(128)S(1)} %get-tuple-element.30), kind=kOutput, calls=%fused_computation.52 | convolution fusion | flops 252526592 | bytes 4522304 | tf_op jit(solution)/shard_map/dot_general | solution.py:65
  145.9 1.6 copy.125
  151.6 14.2 %fusion.61 = (bf16[3,16,64,256]{3,2,1,0:T(8,128)(2,1)}, f32[3,16,64,256]{3,2,1,0:T(8,128)S(1)}) fusion(f32[16]{0:T(128)S(1)} %broadcast_select_fusion, f32[16,64,256]{2,1,0:T(8,128)} %get-tuple-element.35, f32[3]{0:T(128)S(1)} %compare_convert_fusion, f32[3,16,64,256]{3,2,1,0:T(8,128)} %param.11, f32[3,16,64,256]{3,2,1,0:T(8,128)} %reshape.196, ...), kind=kLoop, calls=%fused_computation.120 | loop fusion | flops 23592960 | bytes 26562636 | tf_op jit(solution)/shard_map/convert.6
  166.6 3.8 %fusion.63 = (f32[3,16,64,255]{3,2,1,0:T(8,128)}, f32[3,16,64,255]{3,2,1,0:T(8,128)}) fusion(f32[3,16,64,256]{3,2,1,0:T(8,128)S(1)} %get-tuple-element.3), kind=kLoop, calls=%fused_computation.122 | loop fusion | bytes 12533760 | tf_op jit(solution)/shard_map/slice | solution.py:96
  170.4 5.8 %copy.137 = bf16[128,2,3,2048]{3,1,0,2:T(2,128)(2,1)} copy(bf16[128,2,3,2048]{3,1,2,0:T(2,128)(2,1)} %all-to-all-done.1) | data formatting | bytes 6291456 | tf_op jit(solution)/shard_map/all_to_all | solution.py:176
  176.2 5.7 %reshape.198 = bf16[256,3,2048]{2,0,1:T(8,128)(2,1)} reshape(bf16[128,2,3,2048]{3,1,0,2:T(2,128)(2,1)} %copy.137) | data formatting | bytes 6291456 | tf_op jit(solution)/shard_map/reshape | solution.py:183
  181.9 4.0 %fusion.5 = (f32[2048,128]{1,0:T(8,128)}, bf16[3,2048,128]{2,1,0:T(8,128)(2,1)S(1)}) fusion(bf16[256,3,2048]{2,0,1:T(8,128)(2,1)} %reshape.198, s32[128]{0:T(128)S(1)} %copy-done.8), kind=kOutput, calls=%fused_computation.13 | convolution fusion | flops 405569536 | bytes 5767680 | tf_op jit(solution)/shard_map/jr,rcb->cjb/dot_general | solution.py:184
  186.2 2.3 slice_multiply_fusion.2
  188.4 2.5 copy.149
  191.0 2.4 mul.428
  196.0 2.5 copy.148
  198.6 2.4 mul.422
  200.9 1.7 slice_multiply_fusion.1
  204.0 67.2 %psum.16 = f32[80]{0:T(128)S(1)} all-reduce(f32[80]{0:T(128)S(1)} %select_add_fusion), channel_id=1, replica_groups=mesh['gx'=64,'gy'=2] {'gx','gy'}, use_global_device_ids=true, to_apply=%region_6.7 | all-reduce | flops 80 | bytes 640 | tf_op jit(solution)/shard_map/psum | solution.py:200
  272.0 2.4 collective-permute-start.5
  274.4 2.5 copy.139
  277.0 2.4 mul.395
  279.3 2.5 multiply_bitcast_fusion
  281.9 2.7 bitcast_multiply_fusion
  284.6 3.5 %concatenate.83 = bf16[3,16,64,2,128]{4,3,2,1,0:T(2,128)(2,1)} reshape(bf16[3,16,64,256]{3,2,1,0:T(8,128)(2,1)} %get-tuple-element.2) | data formatting | bytes 3145728 | tf_op jit(solution)/shard_map/concatenate | solution.py:27
  288.1 4.4 %copy.144 = bf16[3,16,64,2,128]{4,1,3,2,0:T(8,128)(2,1)} copy(bf16[3,16,64,2,128]{4,3,2,1,0:T(2,128)(2,1)} %concatenate.83) | data formatting | bytes 3145728 | tf_op jit(solution)/shard_map/concatenate | solution.py:27
  292.5 2.5 copy.140
  295.0 2.4 mul.398
  297.4 2.5 copy.141
  299.9 2.4 mul.401
  302.3 2.5 copy.142
  304.8 2.4 mul.409
  314.1 5.6 %bitcast_convert_fusion = bf16[16,2,8,3,64,128]{5,2,4,3,1,0:T(8,128)(2,1)S(1)} fusion(bf16[3,1,64,2,128]{4,1,3,2,0:T(2,128)(2,1)} %concatenate.89, bf16[3,16,64,2,128]{4,1,3,2,0:T(8,128)(2,1)} %copy.144, bf16[3,1,64,2,128]{4,1,3,2,0:T(2,128)(2,1)} %concatenate.88, s32[18,2]{0,1:T(2,128)S(1)} %multiply_add_fusion, s32[16,2,8]{2,1,0:T(2,128)S(1)} %bitcast.123), kind=kOutput, calls=%fused_computation | convolution fusion | flops 464593920 | bytes 14353552 | tf_op jit(solution)/shard_map/xbkqc,aqycz->xbkayz/dot_general | solution.py:117
  319.7 3.4 %fusion.17 = f32[3,16,64,2,128]{4,2,0,3,1:T(8,128)S(1)} fusion(bf16[16,2,8,3,64,128]{5,2,4,3,1,0:T(8,128)(2,1)S(1)} %bitcast_convert_fusion, bf16[8,128,128]{2,1,0:T(8,128)(2,1)S(1)} %copy-done), kind=kOutput, calls=%fused_computation.41 | convolution fusion | flops 1610612736 | bytes 15990784 | tf_op jit(solution)/shard_map/xbkayz,kzw->axybw/dot_general | solution.py:120
  323.1 4.4 %copy.147 = f32[3,16,64,2,128]{4,3,2,1,0:T(2,128)} copy(f32[3,16,64,2,128]{4,2,0,3,1:T(8,128)S(1)} %fusion.17) | data formatting | bytes 6291456 | tf_op jit(solution)/shard_map/xbkayz,kzw->axybw/transpose | solution.py:120
  327.6 5.5 %reshape.199 = f32[3,16,64,256]{3,2,1,0:T(8,128)} reshape(f32[3,16,64,2,128]{4,3,2,1,0:T(2,128)} %copy.147) | data formatting | bytes 6291456 | tf_op jit(solution)/shard_map/reshape | solution.py:123
  333.1 9.4 %subtract_multiply_fusion = f32[3,16,64,256]{3,2,1,0:T(8,128)} fusion(f32[3,16,64,256]{3,2,1,0:T(8,128)S(1)} %get-tuple-element.3, f32[3,16,64,256]{3,2,1,0:T(8,128)} %reshape.199, f32[3,16,64,255]{3,2,1,0:T(8,128)} %get-tuple-element.17, f32[3,16,64,255]{3,2,1,0:T(8,128)} %get-tuple-element.16, f32[3,18,1,256]{3,2,1,0:T(1,128)} %collective-permute-done.6, ...), kind=kLoop, calls=%fused_computation.26 | loop fusion | flops 25952256 | bytes 21450828 | tf_op jit(solution)/shard_map/mul | solution.py:128
  (81 shorter events, 24.4 us)
Async XLA Ops:
  0.6 87.7 %copy-start = (bf16[8,128,128]{2,1,0:T(8,128)(2,1)S(1)}, bf16[8,128,128]{2,1,0:T(8,128)(2,1)}, u32[]{:S(2)}) copy-start(bf16[8,128,128]{2,1,0:T(8,128)(2,1)} %param.16) | copy-start | bytes 786436
  15.6 11.9 %copy-start.1 = (f32[3,16,64,256]{3,2,1,0:T(8,128)S(1)}, f32[3,16,64,256]{3,2,1,0:T(8,128)}, u32[]{:S(2)}) copy-start(f32[3,16,64,256]{3,2,1,0:T(8,128)} %param.11) | copy-start | bytes 9437188
  15.6 91.2 %all-to-all-start = ((bf16[128,2,3,2048]{3,1,2,0:T(2,128)(2,1)}), bf16[128,2,3,2048]{3,1,2,0:T(2,128)(2,1)}, u32[]{:S(2)}, u32[]{:S(2)}) async-start(bf16[128,2,3,2048]{3,1,2,0:T(2,128)(2,1)} %copy.121), calls=%async_computation | async-start | bytes 6291456 | tf_op jit(solution)/shard_map/all_to_all | solution.py:176
  28.3 38.3 %collective-permute-start.1 = (f32[3,1,64,256]{3,2,1,0:T(8,128)}, f32[3,1,64,256]{3,2,1,0:T(8,128)}, u32[]{:S(2)}, u32[]{:S(2)}) collective-permute-start(f32[3,1,64,256]{3,2,1,0:T(8,128)} %get-tuple-element.24), channel_id=1, source_target_pairs={{0,2},{2,4},{4,6},{6,8},{8,10},{10,12},{12,14},{14,16},{16,18},{18... | collective-permute-start | bytes 589832 | tf_op jit(solution)/shard_map/ppermute | solution.py:23
  31.8 39.0 %collective-permute-start = (f32[3,1,64,256]{3,2,1,0:T(8,128)}, f32[3,1,64,256]{3,2,1,0:T(8,128)}, u32[]{:S(2)}, u32[]{:S(2)}) collective-permute-start(f32[3,1,64,256]{3,2,1,0:T(8,128)} %get-tuple-element.25), channel_id=1, source_target_pairs={{2,0},{4,2},{6,4},{8,6},{10,8},{12,10},{14,12},{16,14},{18,16},{20... | collective-permute-start | bytes 589832 | tf_op jit(solution)/shard_map/ppermute | solution.py:26
  32.0 3.8 %copy-start.6 = (bf16[2,128,3,2048]{3,1,2,0:T(8,128)(2,1)S(1)}, bf16[2,128,3,2048]{3,1,2,0:T(8,128)(2,1)}, u32[]{:S(2)}) copy-start(bf16[2,128,3,2048]{3,1,2,0:T(8,128)(2,1)} %param.12) | copy-start | bytes 9437188
  35.8 2.7 copy-start.11
  35.8 6.0 %copy-start.12 = (f32[80]{0:T(128)S(1)}, f32[80]{0:T(128)}, u32[]{:S(2)}) copy-start(f32[80]{0:T(128)} %param.18) | copy-start | bytes 964
  35.8 6.0 %copy-start.9 = (s32[80]{0:T(128)S(1)}, s32[80]{0:T(128)}, u32[]{:S(2)}) copy-start(s32[80]{0:T(128)} %param.20) | copy-start | bytes 964
  35.8 6.0 %copy-start.10 = (f32[80]{0:T(128)S(1)}, f32[80]{0:T(128)}, u32[]{:S(2)}) copy-start(f32[80]{0:T(128)} %param.17) | copy-start | bytes 964
  35.8 9.8 %copy-start.7 = (s32[32,8]{0,1:T(8,128)S(1)}, s32[32,8]{0,1:T(8,128)}, u32[]{:S(2)}) copy-start(s32[32,8]{0,1:T(8,128)} %param.15) | copy-start | bytes 3076
  51.7 5.7 %copy-start.13 = (s32[128]{0:T(128)S(1)}, s32[128]{0:T(128)}, u32[]{:S(2)}) copy-start(s32[128]{0:T(128)} %param.21) | copy-start | bytes 1540
  103.7 48.0 %collective-permute-start.2 = (f32[3,18,1,256]{3,2,1,0:T(1,128)}, f32[3,18,1,256]{3,2,1,0:T(1,128)S(1)}, u32[]{:S(2)}, u32[]{:S(2)}) collective-permute-start(f32[3,18,1,256]{3,2,1,0:T(1,128)} %get-tuple-element.6), channel_id=1, source_target_pairs={{1,0},{0,1},{3,2},{2,3},{5,4},{4,5},{7,6},{6,7},{9,8},{8,9},{11,10... | collective-permute-start | bytes 165896 | tf_op jit(solution)/shard_map/ppermute | solution.py:26
  106.7 44.9 %collective-permute-start.3 = (f32[3,18,1,256]{3,2,1,0:T(1,128)}, f32[3,18,1,256]{3,2,1,0:T(1,128)}, u32[]{:S(2)}, u32[]{:S(2)}) collective-permute-start(f32[3,18,1,256]{3,2,1,0:T(1,128)} %get-tuple-element.7), channel_id=1, source_target_pairs={{0,1},{1,0},{2,3},{3,2},{4,5},{5,4},{6,7},{7,6},{8,9},{9,8},{10,11... | collective-permute-start | bytes 165896 | tf_op jit(solution)/shard_map/ppermute | solution.py:23
  106.7 63.7 %all-to-all-start.1 = ((bf16[128,2,3,2048]{3,1,2,0:T(2,128)(2,1)}), bf16[128,2,3,2048]{3,1,2,0:T(2,128)(2,1)}, u32[]{:S(2)}, u32[]{:S(2)}) async-start(bf16[128,2,3,2048]{3,1,2,0:T(2,128)(2,1)} %copy.136), calls=%async_computation.1 | async-start | bytes 6291456 | tf_op jit(solution)/shard_map/all_to_all | solution.py:176
  122.7 5.7 %copy-start.8 = (s32[128]{0:T(128)S(1)}, s32[128]{0:T(128)}, u32[]{:S(2)}) copy-start(s32[128]{0:T(128)} %param.14) | copy-start | bytes 1540
  145.9 2.8 copy-start.4
  147.5 2.6 copy-start.5
  193.3 1.4 copy-start.2
  200.9 1.7 copy-start.3
  271.2 36.7 %collective-permute-start.4 = (f32[3,1,64,256]{3,2,1,0:T(8,128)}, f32[3,1,64,256]{3,2,1,0:T(8,128)}, u32[]{:S(2)}, u32[]{:S(2)}) collective-permute-start(f32[3,1,64,256]{3,2,1,0:T(8,128)} %get-tuple-element.19), channel_id=1, source_target_pairs={{2,0},{4,2},{6,4},{8,6},{10,8},{12,10},{14,12},{16,14},{18,16},{20... | collective-permute-start | bytes 589832 | tf_op jit(solution)/shard_map/ppermute | solution.py:26
  272.0 35.8 %collective-permute-start.5 = (f32[3,1,64,256]{3,2,1,0:T(8,128)}, f32[3,1,64,256]{3,2,1,0:T(8,128)}, u32[]{:S(2)}, u32[]{:S(2)}) collective-permute-start(f32[3,1,64,256]{3,2,1,0:T(8,128)} %get-tuple-element.18), channel_id=1, source_target_pairs={{0,2},{2,4},{4,6},{6,8},{8,10},{10,12},{12,14},{14,16},{16,18},{18... | collective-permute-start | bytes 589832 | tf_op jit(solution)/shard_map/ppermute | solution.py:23
  309.3 23.7 %collective-permute-start.6 = (f32[3,18,1,256]{3,2,1,0:T(1,128)}, f32[3,18,1,256]{3,2,1,0:T(1,128)}, u32[]{:S(2)}, u32[]{:S(2)}) collective-permute-start(f32[3,18,1,256]{3,2,1,0:T(1,128)} %get-tuple-element.5), channel_id=1, source_target_pairs={{1,0},{0,1},{3,2},{2,3},{5,4},{4,5},{7,6},{6,7},{9,8},{8,9},{11,10... | collective-permute-start | bytes 165896 | tf_op jit(solution)/shard_map/ppermute | solution.py:26
  309.3 23.7 %collective-permute-start.7 = (f32[3,18,1,256]{3,2,1,0:T(1,128)}, f32[3,18,1,256]{3,2,1,0:T(1,128)}, u32[]{:S(2)}, u32[]{:S(2)}) collective-permute-start(f32[3,18,1,256]{3,2,1,0:T(1,128)} %get-tuple-element.4), channel_id=1, source_target_pairs={{0,1},{1,0},{2,3},{3,2},{4,5},{5,4},{6,7},{7,6},{8,9},{9,8},{10,11... | collective-permute-start | bytes 165896 | tf_op jit(solution)/shard_map/ppermute | solution.py:23
where the time goes:
time: 349 us; the launch traced here: 343 us
  local copies, waits for them, and re-layouts  138 us (40%)
  blocking collectives  67.2 us (19%)
  other arithmetic  54.9 us (16%)
  matrix products  39 us (11%)
  starting transfers between devices  33.5 us (10%)
  waiting for transfers between devices  8.97 us (3%)
    psum x1, blocking collectives, shards(): gradient_sum = gradient_sum + lax.psum(gradient_part, ('gx', 'gy'))  67.2 us
    all_to_all x2, starting transfers between devices, shards(): lax.all_to_all(packed.reshape((tile_count, CAP) + block_shape), ('gx', 'g...  22 us
    reshape x4, local copies, waits for them, and re-layouts, shards(): packed.reshape((tile_count, CAP) + block_shape)  20.1 us
    concatenate x8, local copies, waits for them, and re-layouts, padded(): block = jnp.concatenate([low, block, high], axis=dim)  19.5 us
    another operation x3, other arithmetic  16.1 us
    all_to_all x2, local copies, waits for them, and re-layouts, shards(): lax.all_to_all(packed.reshape((tile_count, CAP) + block_shape), ('gx', 'g...  11.7 us
    reshape x2, local copies, waits for them, and re-layouts, shards(): arrived = arrived.reshape((tile_count * CAP,) + block_shape)  11.4 us
    dot_general x2, matrix products, advance(): jnp.einsum('xbkqc,aqycz->xbkayz', selector, planes, preferred_element_typ...  11.2 us
  transfers between devices with their start and end apart: 10, of which 1 were waited for; matrix products, arithmetic and copies ran while one was open for 50% of the time, Pallas kernels for 0%

commit v1 on v0

--- a/solution.py
+++ b/solution.py
@@ -197,7 +197,12 @@
             drag_field,
             fringe_scale,
         )
-        gradient_sum = gradient_sum + lax.psum(gradient_part, ("gx", "gy"))
+
+        def lane_touch(q_in, lane_axis):
+            local_part = lax.all_gather(q_in, lane_axis)
+            return jnp.sum(local_part, axis=0)
+
+        gradient_sum = gradient_sum + lane_touch(gradient_part, ("gx", "gy"))
     cosine = jnp.cos(yaw_angle)
     sine = jnp.sin(yaw_angle)
     control_gradient = jnp.stack(

time: 349 us -> 420 us (1.20)
  waiting for transfers between devices: 8.97 us -> 131 us
  blocking collectives: 67.2 us -> 0 us
  between operations: 1.2 us -> 14.6 us
    unnamed x0 -> x2, waiting for transfers between devices: none -> 118 us
    psum x1 -> x0, blocking collectives: 67.2 us -> none  [shards(): gradient_sum = gradient_sum + lax.psum(gradient_part, ('gx', 'gy'))]
  transfers between devices with their start and end apart: 10 -> 11, of which waited for: 1 -> 2; matrix products, arithmetic and copies ran while one was open for 50% -> 44% of each run, Pallas kernels for 0% -> 0%
where the time goes in v1:
time: 420 us; the launch traced here: 414 us
  local copies, waits for them, and re-layouts  141 us (34%)
  waiting for transfers between devices  131 us (31%)
  other arithmetic  54.9 us (13%)
  matrix products  39 us (9%)
  starting transfers between devices  33.4 us (8%)
  between operations  14.6 us (3%)
    unnamed x2, waiting for transfers between devices  118 us
    all_to_all x2, starting transfers between devices, shards(): lax.all_to_all(packed.reshape((tile_count, CAP) + block_shape), ('gx', 'g...  21.4 us
    reshape x4, local copies, waits for them, and re-layouts, shards(): packed.reshape((tile_count, CAP) + block_shape)  20.2 us
    concatenate x8, local copies, waits for them, and re-layouts, padded(): block = jnp.concatenate([low, block, high], axis=dim)  19.6 us
    another operation x3, other arithmetic  16 us
    ppermute x4, waiting for transfers between devices, padded(): lax.ppermute(lax.slice_in_dim(block, block.shape[dim] - width, None, axis...  12.6 us
    reshape x2, local copies, waits for them, and re-layouts, shards(): arrived = arrived.reshape((tile_count * CAP,) + block_shape)  11.8 us
    all_to_all x2, local copies, waits for them, and re-layouts, shards(): lax.all_to_all(packed.reshape((tile_count, CAP) + block_shape), ('gx', 'g...  11.7 us
  transfers between devices with their start and end apart: 11, of which 2 were waited for; matrix products, arithmetic and copies ran while one was open for 44% of the time, Pallas kernels for 0%

profile of v1, /device:TPU:1, one launch (start us, length us, event | category | flops | bytes accessed | tf_op | source)
XLA Modules:
  0.0 413.7 jit_solution(1494674230278963952)
XLA Ops:
  9.6 4.0 convolution_convert_fusion.1
  13.7 4.6 %reshape.194 = bf16[128,2,3,2048]{3,1,0,2:T(2,128)(2,1)S(1)} reshape(bf16[256,3,2048]{2,0,1:T(8,128)(2,1)} %convolution_convert_fusion.1) | data formatting | bytes 6291456 | tf_op jit(solution)/shard_map/reshape | solution.py:177
  18.3 3.8 copy.121
  22.1 11.9 %all-to-all-start = ((bf16[128,2,3,2048]{3,1,2,0:T(2,128)(2,1)}), bf16[128,2,3,2048]{3,1,2,0:T(2,128)(2,1)}, u32[]{:S(2)}, u32[]{:S(2)}) async-start(bf16[128,2,3,2048]{3,1,2,0:T(2,128)(2,1)} %copy.121), calls=%async_computation | async-start | bytes 6291456 | tf_op jit(solution)/shard_map/all_to_all | solution.py:176
  34.8 3.5 collective-permute-start.1
  38.5 3.9 fusion.65
  42.4 2.6 convolution_convert_fusion
  46.3 2.0 mul.377
  48.5 6.0 %reshape.197 = bf16[128,2,3,2048]{3,1,0,2:T(2,128)(2,1)} reshape(bf16[256,3,2048]{2,0,1:T(8,128)(2,1)} %convolution_convert_fusion) | data formatting | bytes 6291456 | tf_op jit(solution)/shard_map/reshape | solution.py:177
  54.5 5.7 %copy.136 = bf16[128,2,3,2048]{3,1,2,0:T(2,128)(2,1)} copy(bf16[128,2,3,2048]{3,1,0,2:T(2,128)(2,1)} %reshape.197) | data formatting | bytes 6291456 | tf_op jit(solution)/shard_map/reshape | solution.py:177
  60.5 12.6 %collective-permute-done.1 = f32[3,1,64,256]{3,2,1,0:T(8,128)} collective-permute-done((f32[3,1,64,256]{3,2,1,0:T(8,128)}, f32[3,1,64,256]{3,2,1,0:T(8,128)}, u32[]{:S(2)}, u32[]{:S(2)}) %collective-permute-start.1) | collective-permute-done | bytes 196640 | tf_op jit(solution)/shard_map/ppermute | solution.py:23
  73.1 1.7 constant_dynamic-update-slice_fusion.2
  74.8 2.6 constant_dynamic-update-slice_fusion.1
  77.3 1.8 constant_dynamic-update-slice_fusion
  79.1 1.6 concatenate.87
  80.8 3.5 concatenate.72
  84.3 4.4 %copy.130 = bf16[3,16,64,2,128]{4,1,3,2,0:T(8,128)(2,1)} copy(bf16[3,16,64,2,128]{4,3,2,1,0:T(2,128)(2,1)} %concatenate.72) | data formatting | bytes 3145728 | tf_op jit(solution)/shard_map/concatenate | solution.py:27
  89.4 5.6 %bitcast_convert_fusion.1 = bf16[16,2,8,3,64,128]{5,2,4,3,1,0:T(8,128)(2,1)S(1)} fusion(bf16[3,1,64,2,128]{4,1,3,2,0:T(2,128)(2,1)} %concatenate.87, bf16[3,16,64,2,128]{4,1,3,2,0:T(8,128)(2,1)} %copy.130, bf16[3,1,64,2,128]{4,1,3,2,0:T(2,128)(2,1)} %concatenate.86, s32[18,2]{0,1:T(2,128)S(1)} %multiply_add_fusion, s32[16,2,8]{2,1,0:T(2,128)S(1)} %bitcast.122), kind=kOutput, calls=%fused_computation.1 | convolution fusion | flops 464593920 | bytes 14353552 | tf_op jit(solution)/shard_map/xbkqc,aqycz->xbkayz/dot_general | solution.py:117
  95.0 3.4 fusion.14
  98.4 4.4 %copy.133 = f32[3,16,64,2,128]{4,3,2,1,0:T(2,128)} copy(f32[3,16,64,2,128]{4,2,0,3,1:T(8,128)S(1)} %fusion.14) | data formatting | bytes 6291456 | tf_op jit(solution)/shard_map/xbkayz,kzw->axybw/transpose | solution.py:120
  102.8 5.5 %reshape.196 = f32[3,16,64,256]{3,2,1,0:T(8,128)} reshape(f32[3,16,64,2,128]{4,3,2,1,0:T(2,128)} %copy.133) | data formatting | bytes 6291456 | tf_op jit(solution)/shard_map/reshape | solution.py:123
  108.3 1.9 fusion.62
  110.2 3.0 collective-permute-start.2
  113.2 9.5 %all-to-all-start.1 = ((bf16[128,2,3,2048]{3,1,2,0:T(2,128)(2,1)}), bf16[128,2,3,2048]{3,1,2,0:T(2,128)(2,1)}, u32[]{:S(2)}, u32[]{:S(2)}) async-start(bf16[128,2,3,2048]{3,1,2,0:T(2,128)(2,1)} %copy.136), calls=%async_computation.1 | async-start | bytes 6291456 | tf_op jit(solution)/shard_map/all_to_all | solution.py:176
  122.8 5.8 %copy.122 = bf16[128,2,3,2048]{3,1,0,2:T(2,128)(2,1)} copy(bf16[128,2,3,2048]{3,1,2,0:T(2,128)(2,1)} %all-to-all-done) | data formatting | bytes 6291456 | tf_op jit(solution)/shard_map/all_to_all | solution.py:176
  128.7 6.1 %reshape.195 = bf16[256,3,2048]{2,0,1:T(8,128)(2,1)} reshape(bf16[128,2,3,2048]{3,1,0,2:T(2,128)(2,1)} %copy.122) | data formatting | bytes 6291456 | tf_op jit(solution)/shard_map/reshape | solution.py:183
  134.8 4.0 fusion.4
  139.0 2.2 slice_multiply_fusion.3
  141.2 2.5 copy.148
  143.7 2.4 mul.422
  149.8 2.0 copy.160
  151.8 2.6 copy.124
  154.3 2.4 mul.349
  156.7 2.5 multiply_bitcast_fusion.1
  159.2 3.8 bitcast_multiply_fusion.1
  162.9 1.6 copy.125
  168.8 14.1 %fusion.61 = (bf16[3,16,64,256]{3,2,1,0:T(8,128)(2,1)}, f32[3,16,64,256]{3,2,1,0:T(8,128)S(1)}) fusion(f32[16]{0:T(128)S(1)} %broadcast_select_fusion, f32[16,64,256]{2,1,0:T(8,128)} %get-tuple-element.39, f32[3]{0:T(128)S(1)} %compare_convert_fusion, f32[3,16,64,256]{3,2,1,0:T(8,128)} %param.11, f32[3,16,64,256]{3,2,1,0:T(8,128)} %reshape.196, ...), kind=kLoop, calls=%fused_computation.121 | loop fusion | flops 23592960 | bytes 26562636 | tf_op jit(solution)/shard_map/convert.6
  183.6 3.8 fusion.63
  187.5 5.8 %copy.137 = bf16[128,2,3,2048]{3,1,0,2:T(2,128)(2,1)} copy(bf16[128,2,3,2048]{3,1,2,0:T(2,128)(2,1)} %all-to-all-done.1) | data formatting | bytes 6291456 | tf_op jit(solution)/shard_map/all_to_all | solution.py:176
  193.3 5.7 %reshape.198 = bf16[256,3,2048]{2,0,1:T(8,128)(2,1)} reshape(bf16[128,2,3,2048]{3,1,0,2:T(2,128)(2,1)} %copy.137) | data formatting | bytes 6291456 | tf_op jit(solution)/shard_map/reshape | solution.py:183
  199.1 4.0 fusion.5
  203.3 2.1 slice_multiply_fusion.2
  205.4 2.5 copy.149
  207.9 2.4 mul.428
  214.2 2.5 collective-permute-start.5
  216.7 2.5 copy.139
  219.2 2.4 mul.395
  221.5 2.5 multiply_bitcast_fusion
  224.8 2.7 bitcast_multiply_fusion
  227.5 3.5 concatenate.83
  231.0 4.4 %copy.144 = bf16[3,16,64,2,128]{4,1,3,2,0:T(8,128)(2,1)} copy(bf16[3,16,64,2,128]{4,3,2,1,0:T(2,128)(2,1)} %concatenate.83) | data formatting | bytes 3145728 | tf_op jit(solution)/shard_map/concatenate | solution.py:27
  235.4 2.5 copy.140
  237.9 2.4 mul.398
  240.3 2.5 copy.141
  242.8 2.4 mul.401
  245.2 2.5 copy.142
  247.7 2.4 mul.409
  250.1 118.2 %all-reduce.9.cloned.1.call-done = (f32[10240]{0:T(1024)}, f32[10240]{0:T(1024)}) async-done(((f32[10240]{0:T(1024)}, f32[10240]{0:T(1024)}), (f32[10240]{0:T(1024)}, f32[10240]{0:T(1024)})) %all-reduce.9.cloned.1.call-update) | async-done | bytes 81936
  372.0 1.5 pad_maximum_fusion.12
  378.3 5.6 %bitcast_convert_fusion = bf16[16,2,8,3,64,128]{5,2,4,3,1,0:T(8,128)(2,1)S(1)} fusion(bf16[3,1,64,2,128]{4,1,3,2,0:T(2,128)(2,1)} %concatenate.89, bf16[3,16,64,2,128]{4,1,3,2,0:T(8,128)(2,1)} %copy.144, bf16[3,1,64,2,128]{4,1,3,2,0:T(2,128)(2,1)} %concatenate.88, s32[18,2]{0,1:T(2,128)S(1)} %copy-done.10, s32[16,2,8]{2,1,0:T(2,128)S(1)} %bitcast.123), kind=kOutput, calls=%fused_computation | convolution fusion | flops 464593920 | bytes 14353552 | tf_op jit(solution)/shard_map/xbkqc,aqycz->xbkayz/dot_general | solution.py:117
  383.9 3.4 fusion.17
  387.3 4.4 %copy.147 = f32[3,16,64,2,128]{4,3,2,1,0:T(2,128)} copy(f32[3,16,64,2,128]{4,2,0,3,1:T(8,128)S(1)} %fusion.17) | data formatting | bytes 6291456 | tf_op jit(solution)/shard_map/xbkayz,kzw->axybw/transpose | solution.py:120
  391.7 5.5 %reshape.199 = f32[3,16,64,256]{3,2,1,0:T(8,128)} reshape(f32[3,16,64,2,128]{4,3,2,1,0:T(2,128)} %copy.147) | data formatting | bytes 6291456 | tf_op jit(solution)/shard_map/reshape | solution.py:123
  397.2 9.4 %subtract_multiply_fusion = f32[3,16,64,256]{3,2,1,0:T(8,128)} fusion(f32[3,16,64,256]{3,2,1,0:T(8,128)S(1)} %get-tuple-element.5, f32[3,16,64,256]{3,2,1,0:T(8,128)} %reshape.199, f32[3,16,64,255]{3,2,1,0:T(8,128)} %get-tuple-element.19, f32[3,16,64,255]{3,2,1,0:T(8,128)} %get-tuple-element.18, f32[3,18,1,256]{3,2,1,0:T(1,128)} %collective-permute-done.6, ...), kind=kLoop, calls=%fused_computation.26 | loop fusion | flops 25952256 | bytes 21450828 | tf_op jit(solution)/shard_map/mul | solution.py:128
  (107 shorter events, 27.9 us)
Async XLA Ops:
  7.2 87.8 %copy-start = (bf16[8,128,128]{2,1,0:T(8,128)(2,1)S(1)}, bf16[8,128,128]{2,1,0:T(8,128)(2,1)}, u32[]{:S(2)}) copy-start(bf16[8,128,128]{2,1,0:T(8,128)(2,1)} %param.16) | copy-start | bytes 786436
  22.1 11.9 %copy-start.1 = (f32[3,16,64,256]{3,2,1,0:T(8,128)S(1)}, f32[3,16,64,256]{3,2,1,0:T(8,128)}, u32[]{:S(2)}) copy-start(f32[3,16,64,256]{3,2,1,0:T(8,128)} %param.11) | copy-start | bytes 9437188
  22.1 91.2 %all-to-all-start = ((bf16[128,2,3,2048]{3,1,2,0:T(2,128)(2,1)}), bf16[128,2,3,2048]{3,1,2,0:T(2,128)(2,1)}, u32[]{:S(2)}, u32[]{:S(2)}) async-start(bf16[128,2,3,2048]{3,1,2,0:T(2,128)(2,1)} %copy.121), calls=%async_computation | async-start | bytes 6291456 | tf_op jit(solution)/shard_map/all_to_all | solution.py:176
  34.8 38.2 %collective-permute-start.1 = (f32[3,1,64,256]{3,2,1,0:T(8,128)}, f32[3,1,64,256]{3,2,1,0:T(8,128)}, u32[]{:S(2)}, u32[]{:S(2)}) collective-permute-start(f32[3,1,64,256]{3,2,1,0:T(8,128)} %get-tuple-element.26), channel_id=1, source_target_pairs={{0,2},{2,4},{4,6},{6,8},{8,10},{10,12},{12,14},{14,16},{16,18},{18... | collective-permute-start | bytes 589832 | tf_op jit(solution)/shard_map/ppermute | solution.py:23
  38.4 39.0 %collective-permute-start = (f32[3,1,64,256]{3,2,1,0:T(8,128)}, f32[3,1,64,256]{3,2,1,0:T(8,128)}, u32[]{:S(2)}, u32[]{:S(2)}) collective-permute-start(f32[3,1,64,256]{3,2,1,0:T(8,128)} %get-tuple-element.27), channel_id=1, source_target_pairs={{2,0},{4,2},{6,4},{8,6},{10,8},{12,10},{14,12},{16,14},{18,16},{20... | collective-permute-start | bytes 589832 | tf_op jit(solution)/shard_map/ppermute | solution.py:26
  38.5 3.9 copy-start.6
  42.4 2.6 copy-start.20
  42.4 126.3 %copy-start.13 = (f32[3]{0:T(128)}, f32[3]{0:T(128)S(1)}, u32[]{:S(2)}) copy-start(f32[3]{0:T(128)S(1)} %compare_convert_fusion) | copy-start | bytes 40
  42.4 5.9 %copy-start.21 = (f32[80]{0:T(128)S(1)}, f32[80]{0:T(128)}, u32[]{:S(2)}) copy-start(f32[80]{0:T(128)} %param.18) | copy-start | bytes 964
  42.4 6.0 %copy-start.11 = (s32[32,8]{0,1:T(8,128)S(1)}, s32[32,8]{0,1:T(8,128)}, u32[]{:S(2)}) copy-start(s32[32,8]{0,1:T(8,128)} %param.15) | copy-start | bytes 3076
  48.4 100.4 %copy-start.19 = (f32[80]{0:T(128)}, f32[80]{0:T(128)S(1)}, u32[]{:S(2)}) copy-start(f32[80]{0:T(128)S(1)} %cos.4) | copy-start | bytes 964
  54.5 5.7 %copy-start.22 = (s32[128]{0:T(128)S(1)}, s32[128]{0:T(128)}, u32[]{:S(2)}) copy-start(s32[128]{0:T(128)} %param.21) | copy-start | bytes 1540
  60.3 29.1 %copy-start.9 = (s32[18,2]{0,1:T(2,128)}, s32[18,2]{0,1:T(2,128)S(1)}, u32[]{:S(2)}) copy-start(s32[18,2]{0,1:T(2,128)S(1)} %multiply_add_fusion) | copy-start | bytes 436
  60.5 108.3 %copy-start.15 = (f32[16]{0:T(128)}, f32[16]{0:T(128)S(1)}, u32[]{:S(2)}) copy-start(f32[16]{0:T(128)S(1)} %broadcast_select_fusion) | copy-start | bytes 196
  110.2 58.6 %collective-permute-start.2 = (f32[3,18,1,256]{3,2,1,0:T(1,128)}, f32[3,18,1,256]{3,2,1,0:T(1,128)S(1)}, u32[]{:S(2)}, u32[]{:S(2)}) collective-permute-start(f32[3,18,1,256]{3,2,1,0:T(1,128)} %get-tuple-element.8), channel_id=1, source_target_pairs={{1,0},{0,1},{3,2},{2,3},{5,4},{4,5},{7,6},{6,7},{9,8},{8,9},{11,10... | collective-permute-start | bytes 165896 | tf_op jit(solution)/shard_map/ppermute | solution.py:26
  113.2 55.5 %collective-permute-start.3 = (f32[3,18,1,256]{3,2,1,0:T(1,128)}, f32[3,18,1,256]{3,2,1,0:T(1,128)}, u32[]{:S(2)}, u32[]{:S(2)}) collective-permute-start(f32[3,18,1,256]{3,2,1,0:T(1,128)} %get-tuple-element.9), channel_id=1, source_target_pairs={{0,1},{1,0},{2,3},{3,2},{4,5},{5,4},{6,7},{7,6},{8,9},{9,8},{10,11... | collective-permute-start | bytes 165896 | tf_op jit(solution)/shard_map/ppermute | solution.py:23
  113.2 74.2 %all-to-all-start.1 = ((bf16[128,2,3,2048]{3,1,2,0:T(2,128)(2,1)}), bf16[128,2,3,2048]{3,1,2,0:T(2,128)(2,1)}, u32[]{:S(2)}, u32[]{:S(2)}) async-start(bf16[128,2,3,2048]{3,1,2,0:T(2,128)(2,1)} %copy.136), calls=%async_computation.1 | async-start | bytes 6291456 | tf_op jit(solution)/shard_map/all_to_all | solution.py:176
  122.8 245.6 %all-reduce.9.cloned.1.call-start = ((), (), s32[]{:S(2)}) async-start(), calls=%async_computation.2 | async-start | bytes 163840
  128.7 6.1 %copy-start.12 = (s32[128]{0:T(128)S(1)}, s32[128]{0:T(128)}, u32[]{:S(2)}) copy-start(s32[128]{0:T(128)} %param.14) | copy-start | bytes 1540
  143.7 5.1 %copy-start.17 = (s32[80]{0:T(128)S(1)}, s32[80]{0:T(128)}, u32[]{:S(2)}) copy-start(s32[80]{0:T(128)} %param.20) | copy-start | bytes 964
  143.7 5.1 %copy-start.18 = (f32[80]{0:T(128)S(1)}, f32[80]{0:T(128)}, u32[]{:S(2)}) copy-start(f32[80]{0:T(128)} %param.17) | copy-start | bytes 964
  146.1 1.4 copy-start.2
  149.0 10.2 %copy-start.7 = (f32[10240]{0:T(1024)}, f32[10240]{0:T(1024)S(1)}, u32[]{:S(2)}) copy-start(f32[10240]{0:T(1024)S(1)} %get-tuple-element.37) | copy-start | bytes 122884
  162.9 2.8 copy-start.4
  164.6 2.7 copy-start.5
  210.3 1.4 copy-start.3
  213.0 159.0 %collective-permute-start.4 = (f32[3,1,64,256]{3,2,1,0:T(8,128)}, f32[3,1,64,256]{3,2,1,0:T(8,128)}, u32[]{:S(2)}, u32[]{:S(2)}) collective-permute-start(f32[3,1,64,256]{3,2,1,0:T(8,128)} %get-tuple-element.21), channel_id=1, source_target_pairs={{2,0},{4,2},{6,4},{8,6},{10,8},{12,10},{14,12},{16,14},{18,16},{20... | collective-permute-start | bytes 589832 | tf_op jit(solution)/shard_map/ppermute | solution.py:26
  214.2 157.8 %collective-permute-start.5 = (f32[3,1,64,256]{3,2,1,0:T(8,128)}, f32[3,1,64,256]{3,2,1,0:T(8,128)}, u32[]{:S(2)}, u32[]{:S(2)}) collective-permute-start(f32[3,1,64,256]{3,2,1,0:T(8,128)} %get-tuple-element.20), channel_id=1, source_target_pairs={{0,2},{2,4},{4,6},{6,8},{8,10},{10,12},{12,14},{14,16},{16,18},{18... | collective-permute-start | bytes 589832 | tf_op jit(solution)/shard_map/ppermute | solution.py:23
  224.1 0.6 copy-start.8
  370.6 7.6 %copy-start.10 = (s32[18,2]{0,1:T(2,128)S(1)}, s32[18,2]{0,1:T(2,128)}, u32[]{:S(2)}) copy-start(s32[18,2]{0,1:T(2,128)} %copy-done.9) | copy-start | bytes 436
  373.5 23.7 %collective-permute-start.6 = (f32[3,18,1,256]{3,2,1,0:T(1,128)}, f32[3,18,1,256]{3,2,1,0:T(1,128)}, u32[]{:S(2)}, u32[]{:S(2)}) collective-permute-start(f32[3,18,1,256]{3,2,1,0:T(1,128)} %get-tuple-element.7), channel_id=1, source_target_pairs={{1,0},{0,1},{3,2},{2,3},{5,4},{4,5},{7,6},{6,7},{9,8},{8,9},{11,10... | collective-permute-start | bytes 165896 | tf_op jit(solution)/shard_map/ppermute | solution.py:26
  374.8 22.4 %collective-permute-start.7 = (f32[3,18,1,256]{3,2,1,0:T(1,128)}, f32[3,18,1,256]{3,2,1,0:T(1,128)}, u32[]{:S(2)}, u32[]{:S(2)}) collective-permute-start(f32[3,18,1,256]{3,2,1,0:T(1,128)} %get-tuple-element.6), channel_id=1, source_target_pairs={{0,1},{1,0},{2,3},{3,2},{4,5},{5,4},{6,7},{7,6},{8,9},{9,8},{10,11... | collective-permute-start | bytes 165896 | tf_op jit(solution)/shard_map/ppermute | solution.py:23
  391.7 5.5 %copy-start.14 = (f32[3]{0:T(128)S(1)}, f32[3]{0:T(128)}, u32[]{:S(2)}) copy-start(f32[3]{0:T(128)} %copy-done.13) | copy-start | bytes 40
  391.7 5.5 %copy-start.16 = (f32[16]{0:T(128)S(1)}, f32[16]{0:T(128)}, u32[]{:S(2)}) copy-start(f32[16]{0:T(128)} %copy-done.15) | copy-start | bytes 196
Sparse Core Ops, SparseCore 0:
  224.9 143.4 all-reduce.8
